TPU v7x, 32 devices: a whole 2x2x4 slice. The times are simulated.
32 devices in a mesh: seq: 8 (over y, x, core), tp: 4 (over z).
Axes of the slice: x: 2, y: 2, z: 4, core: 2. Of those that a mesh axis runs over, the one named last changes fastest.
Arguments:
- tokens: bfloat16 [1, 4096, 2048], P(None, 'seq'), may hold values from -6 to 6
- gain_attn: float32 [2048], replicated, may hold values from 0.5 to 1.5
- w_query: bfloat16 [2048, 2048], P(None, 'tp'), may hold values from -0.21875 to 0.21875
- w_key: bfloat16 [2048, 2048], P(None, 'tp'), may hold values from -0.21875 to 0.21875
- w_value: bfloat16 [2048, 2048], P(None, 'tp'), may hold values from -0.125 to 0.125
- w_out: bfloat16 [2048, 2048], P('tp'), may hold values from -0.25 to 0.25
- gain_ffn: float32 [2048], replicated, may hold values from 0.5 to 1.5
- w_gate: bfloat16 [2048, 8192], P(None, 'tp'), may hold values from -0.125 to 0.125
- w_up: bfloat16 [2048, 8192], P(None, 'tp'), may hold values from -0.125 to 0.125
- w_down: bfloat16 [8192, 2048], P('tp'), may hold values from -0.0625 to 0.0625
- cotangent: bfloat16 [1, 4096, 2048], P(None, 'seq'), may hold values from -6 to 6
- doc_ids: int32 [1, 4096], replicated, may hold values from 0 to 15, never falling along the last dimension, each value on 1 to 2048 neighbouring positions
- valid: int32 [1, 4096], replicated, may hold values 0 or 1
- group_order: int32 [1, 16], replicated, may hold values from 0 to 15, each once within a row
Outputs:
- layer_out: bfloat16 [1, 4096, 2048], P(None, 'seq')
- grad_tokens: float32 [1, 4096, 2048], P(None, 'seq')
- grad_gain_attn: float32 [2048], P('seq')
- grad_query: float32 [2048, 2048], P('seq', 'tp')
- grad_key: float32 [2048, 2048], P('seq', 'tp')
- grad_value: float32 [2048, 2048], P('seq', 'tp')
- grad_out: float32 [2048, 2048], P('tp', 'seq')
- grad_gain_ffn: float32 [2048], P('seq')
- grad_gate: float32 [2048, 8192], P('seq', 'tp')
- grad_up: float32 [2048, 8192], P('seq', 'tp')
- grad_down: float32 [8192, 2048], P('tp', 'seq')
Inputs may be any that keep to these rules, and one draw needn't show every extreme that they name: `doc_ids`: document numbers never fall along a sequence; a document holds 1 to 2048 positions. `group_order`: each row is a permutation; device i of seq stores storage blocks 2 i and 2 i + 1 of every sequence.
All inputs are finite; a program needn't handle non-finite values.
Results may differ from a plain program's by a relative error of at most 0.014.
The roundings to bfloat16 on the way count: a program that leaves them out, or rounds other values in their place, can miss the bound.
Values may be sent and summed in bfloat16 or wider, within the bound.
No kernel may reach another device: no remote copies, remote signals or barrier semaphores. Data moves between devices by JAX's collectives and lax.ppermute only.
A program may use at most 320 MiB of HBM per device.

v0:
```python
import math
import jax
import jax.numpy as jnp
from jax import lax
from jax.sharding import PartitionSpec as P

HEAD_WIDTH = 128
norm_eps = 1e-05
rope_base = 10000.0


def rope_tables(places, head_size):
    half_size = head_size // 2
    freqs = rope_base ** (-jnp.arange(half_size, dtype=jnp.float32) * 2.0 / head_size)
    angles = places.astype(jnp.float32)[..., None] * freqs
    return (jnp.cos(angles), jnp.sin(angles))


def rotate(values, cosine, sine, forward):
    half_size = values.shape[-1] // 2
    first = values[..., :half_size]
    second = values[..., half_size:]
    cos_b = cosine[..., None, :]
    sin_b = sine[..., None, :]
    if forward:
        return jnp.concatenate(
            [first * cos_b - second * sin_b, second * cos_b + first * sin_b], axis=-1
        )
    return jnp.concatenate(
        [first * cos_b + second * sin_b, second * cos_b - first * sin_b], axis=-1
    )


def visible(place_q, doc_q, place_k, doc_k, live_k):
    allowed = (
        (place_k[None, :] <= place_q[:, None])
        & (doc_k[None, :] == doc_q[:, None])
        & (live_k[None, :] == 1)
    )
    return allowed.astype(jnp.float32)


def score_block(query_heads, key_heads, head_size, length):
    scores = jnp.einsum("qhe,khe->hqk", query_heads, key_heads, preferred_element_type=jnp.float32)
    return scores * (1.0 / math.sqrt(head_size)) - math.log(length)


def score_grads(query_heads, key_heads, value_heads, grad_heads, mask, head_size, length):
    sigma = jax.nn.sigmoid(score_block(query_heads, key_heads, head_size, length))
    weights = (sigma * mask).astype(jnp.bfloat16)
    grad_weights = jnp.einsum(
        "qhe,khe->hqk", grad_heads, value_heads, preferred_element_type=jnp.float32
    )
    grad_scores = (grad_weights * (sigma * (1.0 - sigma)) * mask).astype(jnp.bfloat16)
    return (weights, grad_scores)


def local(
    tokens,
    gain_attn,
    w_query,
    w_key,
    w_value,
    w_out,
    gain_ffn,
    w_gate,
    w_up,
    w_down,
    cotangent,
    doc_ids,
    valid,
    group_order,
):
    seq_count, row_count, model_width = tokens.shape
    length = doc_ids.shape[1]
    span = length // group_order.shape[1]
    head_size = HEAD_WIDTH
    local_width = w_query.shape[1]
    local_heads = local_width // head_size
    flat_rows = seq_count * row_count
    factor = 1.0 / math.sqrt(head_size)
    own_rows = lax.axis_index("seq") * row_count + jnp.arange(row_count, dtype=jnp.int32)
    all_rows = jnp.arange(length, dtype=jnp.int32)
    place_all = jnp.take(group_order, all_rows // span, axis=1) * span + (all_rows % span)[None, :]
    place_own = jnp.take(group_order, own_rows // span, axis=1) * span + (own_rows % span)[None, :]
    doc_all = jnp.take_along_axis(doc_ids, place_all, axis=1)
    live_all = jnp.take_along_axis(valid, place_all, axis=1)
    doc_own = jnp.take_along_axis(doc_ids, place_own, axis=1)
    cosine, sine = rope_tables(place_own, head_size)
    input_rows = tokens.astype(jnp.float32).reshape(flat_rows, model_width)
    scale_attn = lax.rsqrt(jnp.mean(input_rows * input_rows, axis=-1, keepdims=True) + norm_eps)
    unit_attn = input_rows * scale_attn
    normed_attn = (unit_attn * gain_attn).astype(jnp.bfloat16)

    def project(weight_matrix):
        return jnp.dot(normed_attn, weight_matrix, preferred_element_type=jnp.float32).reshape(
            seq_count, row_count, local_heads, head_size
        )

    query_rot = (
        rotate(project(w_query), cosine, sine, True)
        .astype(jnp.bfloat16)
        .reshape(seq_count, row_count, local_width)
    )
    key_rot = (
        rotate(project(w_key), cosine, sine, True)
        .astype(jnp.bfloat16)
        .reshape(seq_count, row_count, local_width)
    )
    value_low = (
        jnp.dot(normed_attn, w_value, preferred_element_type=jnp.float32)
        .astype(jnp.bfloat16)
        .reshape(seq_count, row_count, local_width)
    )
    key_all, value_all = (
        lax.all_gather(key_rot, "seq", axis=1, tiled=True),
        lax.all_gather(value_low, "seq", axis=1, tiled=True),
    )

    def attend(items):
        query_seq, key_seq, value_seq, place_q, doc_q, place_k, doc_k, live_k = items
        query_heads = query_seq.reshape(row_count, local_heads, head_size)
        key_heads = key_seq.reshape(length, local_heads, head_size)
        value_heads = value_seq.reshape(length, local_heads, head_size)
        mask = visible(place_q, doc_q, place_k, doc_k, live_k)
        weights = (
            jax.nn.sigmoid(score_block(query_heads, key_heads, head_size, length)) * mask
        ).astype(jnp.bfloat16)
        mixed = jnp.einsum("hqk,khe->qhe", weights, value_heads, preferred_element_type=jnp.float32)
        return mixed.astype(jnp.bfloat16).reshape(row_count, local_width)

    attention_output = lax.map(
        attend, (query_rot, key_all, value_all, place_own, doc_own, place_all, doc_all, live_all)
    )
    attended_flat = attention_output.reshape(flat_rows, local_width)
    branch_attn = lax.psum(jnp.dot(attended_flat, w_out, preferred_element_type=jnp.float32), "tp")
    hidden_rows = input_rows + branch_attn
    scale_ffn = lax.rsqrt(jnp.mean(hidden_rows * hidden_rows, axis=-1, keepdims=True) + norm_eps)
    unit_ffn = hidden_rows * scale_ffn
    normalized_feedforward = (unit_ffn * gain_ffn).astype(jnp.bfloat16)
    gate_rows = jnp.dot(normalized_feedforward, w_gate, preferred_element_type=jnp.float32)
    up_projected = jnp.dot(normalized_feedforward, w_up, preferred_element_type=jnp.float32)
    gate_sig = jax.nn.sigmoid(gate_rows)
    activation_rows = (gate_rows * gate_sig * up_projected).astype(jnp.bfloat16)
    branch_ffn = lax.psum(
        jnp.dot(activation_rows, w_down, preferred_element_type=jnp.float32).astype(jnp.bfloat16),
        "tp",
    ).astype(jnp.float32)
    layer_out = (
        (hidden_rows + branch_ffn).astype(jnp.bfloat16).reshape(seq_count, row_count, model_width)
    )
    upstream = cotangent.astype(jnp.float32).reshape(flat_rows, model_width)
    upstream_low = upstream.astype(jnp.bfloat16)
    grad_down = jnp.einsum(
        "tf,td->fd", activation_rows, upstream_low, preferred_element_type=jnp.float32
    )
    grad_act = jnp.einsum("td,fd->tf", upstream_low, w_down, preferred_element_type=jnp.float32)
    gate_pre = (grad_act * up_projected * (gate_sig * (1.0 + gate_rows * (1.0 - gate_sig)))).astype(
        jnp.bfloat16
    )
    up_pre = (grad_act * (gate_rows * gate_sig)).astype(jnp.bfloat16)
    grad_gate = jnp.einsum(
        "td,tf->df", normalized_feedforward, gate_pre, preferred_element_type=jnp.float32
    )
    grad_up = jnp.einsum(
        "td,tf->df", normalized_feedforward, up_pre, preferred_element_type=jnp.float32
    )
    normed_ffn_part = jnp.einsum(
        "tf,df->td", gate_pre, w_gate, preferred_element_type=jnp.float32
    ) + jnp.einsum("tf,df->td", up_pre, w_up, preferred_element_type=jnp.float32)
    grad_normed_ffn = lax.psum(normed_ffn_part, "tp")
    gain_ffn_part = jnp.sum(grad_normed_ffn * unit_ffn, axis=0)
    back_ffn = grad_normed_ffn * gain_ffn
    grad_middle = upstream + scale_ffn * (
        back_ffn - unit_ffn * jnp.mean(back_ffn * unit_ffn, axis=-1, keepdims=True)
    )
    middle_low = grad_middle.astype(jnp.bfloat16)
    grad_out = jnp.einsum(
        "te,td->ed", attended_flat, middle_low, preferred_element_type=jnp.float32
    )
    grad_attended = (
        jnp.einsum("td,ed->te", middle_low, w_out, preferred_element_type=jnp.float32)
        .astype(jnp.bfloat16)
        .reshape(seq_count, row_count, local_width)
    )
    key_back, value_back = (key_all, value_all)

    def attend_back(items):
        query_seq, key_seq, value_seq, grad_seq, place_q, doc_q, place_k, doc_k, live_k = items
        query_heads = query_seq.reshape(row_count, local_heads, head_size)
        key_heads = key_seq.reshape(length, local_heads, head_size)
        value_heads = value_seq.reshape(length, local_heads, head_size)
        grad_heads = grad_seq.reshape(row_count, local_heads, head_size)
        mask = visible(place_q, doc_q, place_k, doc_k, live_k)
        weights, grad_scores = score_grads(
            query_heads, key_heads, value_heads, grad_heads, mask, head_size, length
        )
        grad_value_seq = jnp.einsum(
            "hqk,qhe->khe", weights, grad_heads, preferred_element_type=jnp.float32
        )
        grad_query_seq = (
            jnp.einsum("hqk,khe->qhe", grad_scores, key_heads, preferred_element_type=jnp.float32)
            * factor
        )
        grad_key_seq = (
            jnp.einsum("hqk,qhe->khe", grad_scores, query_heads, preferred_element_type=jnp.float32)
            * factor
        )
        return (
            grad_query_seq,
            grad_key_seq.reshape(length, local_width),
            grad_value_seq.reshape(length, local_width),
        )

    grad_query_rot, grad_key_all, grad_value_all = lax.map(
        attend_back,
        (
            query_rot,
            key_back,
            value_back,
            grad_attended,
            place_own,
            doc_own,
            place_all,
            doc_all,
            live_all,
        ),
    )
    grad_key_rot, grad_value_own = (
        lax.psum_scatter(grad_key_all, "seq", scatter_dimension=1, tiled=True),
        lax.psum_scatter(grad_value_all, "seq", scatter_dimension=1, tiled=True),
    )
    query_low = (
        rotate(grad_query_rot, cosine, sine, False)
        .astype(jnp.bfloat16)
        .reshape(flat_rows, local_width)
    )
    key_low = (
        rotate(
            grad_key_rot.reshape(seq_count, row_count, local_heads, head_size), cosine, sine, False
        )
        .astype(jnp.bfloat16)
        .reshape(flat_rows, local_width)
    )
    value_grad_low = grad_value_own.astype(jnp.bfloat16).reshape(flat_rows, local_width)
    grad_query = jnp.einsum("td,te->de", normed_attn, query_low, preferred_element_type=jnp.float32)
    grad_key = jnp.einsum("td,te->de", normed_attn, key_low, preferred_element_type=jnp.float32)
    grad_value = jnp.einsum(
        "td,te->de", normed_attn, value_grad_low, preferred_element_type=jnp.float32
    )
    normed_attn_part = (
        jnp.einsum("te,de->td", query_low, w_query, preferred_element_type=jnp.float32)
        + jnp.einsum("te,de->td", key_low, w_key, preferred_element_type=jnp.float32)
        + jnp.einsum("te,de->td", value_grad_low, w_value, preferred_element_type=jnp.float32)
    )
    grad_normed_attn = lax.psum(normed_attn_part, "tp")
    gain_attn_part = jnp.sum(grad_normed_attn * unit_attn, axis=0)
    back_attn = grad_normed_attn * gain_attn
    grad_inputs = grad_middle + scale_attn * (
        back_attn - unit_attn * jnp.mean(back_attn * unit_attn, axis=-1, keepdims=True)
    )
    grad_tokens = grad_inputs.reshape(seq_count, row_count, model_width)
    (
        query_shard,
        key_shard,
        value_shard,
        out_shard,
        gain_attn_shard,
        gate_shard,
        up_shard,
        down_shard,
        gain_ffn_shard,
    ) = (
        lax.psum_scatter(grad_query, "seq", scatter_dimension=0, tiled=True),
        lax.psum_scatter(grad_key, "seq", scatter_dimension=0, tiled=True),
        lax.psum_scatter(grad_value, "seq", scatter_dimension=0, tiled=True),
        lax.psum_scatter(grad_out, "seq", scatter_dimension=1, tiled=True),
        lax.psum_scatter(gain_attn_part, "seq", scatter_dimension=0, tiled=True),
        lax.psum_scatter(grad_gate, "seq", scatter_dimension=0, tiled=True),
        lax.psum_scatter(grad_up, "seq", scatter_dimension=0, tiled=True),
        lax.psum_scatter(grad_down, "seq", scatter_dimension=1, tiled=True),
        lax.psum_scatter(gain_ffn_part, "seq", scatter_dimension=0, tiled=True),
    )
    return (
        layer_out,
        grad_tokens,
        gain_attn_shard,
        query_shard,
        key_shard,
        value_shard,
        out_shard,
        gain_ffn_shard,
        gate_shard,
        up_shard,
        down_shard,
    )


def solution(mesh):
    placed = (
        P(None, "seq", None),
        P(),
        P(None, "tp"),
        P(None, "tp"),
        P(None, "tp"),
        P("tp", None),
        P(),
        P(None, "tp"),
        P(None, "tp"),
        P("tp", None),
        P(None, "seq", None),
        P(),
        P(),
        P(),
    )
    return jax.shard_map(
        local,
        mesh=mesh,
        in_specs=placed,
        out_specs=(
            P(None, "seq", None),
            P(None, "seq", None),
            P("seq"),
            P("seq", "tp"),
            P("seq", "tp"),
            P("seq", "tp"),
            P("tp", "seq"),
            P("seq"),
            P("seq", "tp"),
            P("seq", "tp"),
            P("tp", "seq"),
        ),
        check_vma=False,
    )
```

profile of v0, /device:TPU:0, one launch (start us, length us, event | category | flops | bytes accessed | tf_op | source)
XLA Modules:
  0.0 1533.5 jit_solution(12664565859678444474)
XLA Ops:
  55.9 23.0 %gather_fusion.1 = s32[4096]{0:T(1024)S(1)} fusion(s32[4096]{0:T(1024)S(1)} %bitcast.181, s32[4096]{0:T(1024)S(1)} %broadcast_clamp_fusion), kind=kCustom, calls=%fused_computation.clone | custom fusion | bytes 49152 | tf_op jit(solution)/shard_map/jit(take_along_axis)/gather | solution.py:86
  79.0 23.0 %gather_fusion.2 = s32[4096]{0:T(1024)S(1)} fusion(s32[4096]{0:T(1024)S(1)} %bitcast.182, s32[4096]{0:T(1024)S(1)} %broadcast_clamp_fusion), kind=kCustom, calls=%fused_computation.1.clone | custom fusion | bytes 49152 | tf_op jit(solution)/shard_map/jit(take_along_axis)/gather | solution.py:87
  106.5 17.4 %add_divide_fusion = f32[4,512,4096]{2,1,0:T(8,128)} fusion(bf16[4096,4,128]{0,2,1:T(8,128)(2,1)} %bitcast.193, bf16[512,4,64]{0,2,1:T(8,128)(2,1)S(1)} %get-tuple-element.103, bf16[512,4,64]{0,2,1:T(8,128)(2,1)S(1)} %get-tuple-element.102), kind=kOutput, calls=%fused_computation.8 | convolution fusion | flops 2190475264 | bytes 38273024 | tf_op jit(solution)/shard_map/while/body/eval_jaxpr/qhe,khe->hqk/dot_general | solution.py:44
  124.0 16.5 %fusion.56 = bf16[4,128,512]{2,1,0:T(8,128)(2,1)S(1)} fusion(f32[4,512,4096]{2,1,0:T(8,128)} %add_divide_fusion, f32[512,4096]{1,0:T(8,128)} %and_convert_fusion, bf16[4096,512]{1,0:T(8,128)(2,1)} %all-gather.6.cloned.1.call-done), kind=kOutput, calls=%fused_computation.74 | convolution fusion | flops 2164523008 | bytes 46661632 | tf_op jit(solution)/shard_map/while/body/eval_jaxpr/hqk,khe->qhe/dot_general | solution.py:129
  145.2 157.1 %all-reduce.8.cloned.1.call-done = f32[512,2048]{1,0:T(8,128)} async-done(((f32[512,2048]{1,0:T(8,128)}), f32[512,2048]{1,0:T(8,128)}) %all-reduce.8.cloned.1.call-update) | async-done | bytes 4194320 | tf_op jit(solution)/shard_map/psum | solution.py:136
  306.2 11.8 fusion.96
  324.3 11.6 multiply_convert_fusion.1
  335.9 8.5 fusion.98
  344.4 9.5 convolution_add_fusion
  354.2 9.8 convolution_convert_fusion
  364.1 144.0 %all-reduce.12.cloned.1.call-done = f32[512,2048]{1,0:T(8,128)} async-done(((f32[512,2048]{1,0:T(8,128)}), f32[512,2048]{1,0:T(8,128)}) %all-reduce.12.cloned.1.call-update) | async-done | bytes 4194320 | tf_op jit(solution)/shard_map/psum | solution.py:171
  512.6 83.9 %all-reduce.10.cloned.1.call-done = bf16[512,2048]{1,0:T(8,128)(2,1)} async-done(((bf16[512,2048]{1,0:T(8,128)(2,1)}), bf16[512,2048]{1,0:T(8,128)(2,1)}) %all-reduce.10.cloned.1.call-update) | async-done | bytes 2097168 | tf_op jit(solution)/shard_map/psum | solution.py:145
  606.3 21.1 %fusion.2 = bf16[4,512,4096]{2,1,0:T(8,128)(2,1)} fusion(f32[4,512,4096]{2,1,0:T(8,128)} %add_divide_fusion, f32[512,4096]{1,0:T(8,128)} %and_convert_fusion, bf16[512,4,128]{0,2,1:T(8,128)(2,1)S(1)} %bitcast.195, bf16[4096,512]{1,0:T(8,128)(2,1)} %all-gather.6.cloned.1.call-done), kind=kOutput, calls=%fused_computation.6 | convolution fusion | flops 2189426688 | bytes 63438848 | tf_op jit(solution)/shard_map/while/body/eval_jaxpr/qhe,khe->hqk/dot_general | solution.py:51
  627.4 11.4 convolution_multiply_fusion
  639.0 21.6 %fusion.26 = f32[4,128,4096]{2,1,0:T(8,128)} fusion(bf16[512,4,128]{0,2,1:T(8,128)(2,1)S(1)} %bitcast.196, f32[4,512,4096]{2,1,0:T(8,128)} %add_divide_fusion, f32[512,4096]{1,0:T(8,128)} %and_convert_fusion), kind=kOutput, calls=%fused_computation.49 | convolution fusion | flops 2164260864 | bytes 50855936 | tf_op jit(solution)/shard_map/while/body/eval_jaxpr/hqk,qhe->khe/dot_general | solution.py:198
  660.8 13.5 fusion.52
  674.3 35.0 %reduce-scatter.10.cloned.1.call-done = f32[1,512,512]{1,2,0:T(8,128)} async-done(((f32[1,4096,512]{1,2,0:T(8,128)}), f32[1,512,512]{1,2,0:T(8,128)}) %reduce-scatter.10.cloned.1.call-update) | async-done | bytes 1048592 | tf_op jit(solution)/shard_map/reduce_scatter | solution.py:230
  717.4 66.6 %reduce-scatter.12.cloned.1.call-done = f32[1,512,512]{1,2,0:T(8,128)} async-done(((f32[1,4096,512]{1,2,0:T(8,128)}), f32[1,512,512]{1,2,0:T(8,128)}) %reduce-scatter.12.cloned.1.call-update) | async-done | bytes 1048592 | tf_op jit(solution)/shard_map/reduce_scatter | solution.py:231
  784.0 7.0 add_add_fusion
  811.4 12.6 fusion.101
  824.1 12.6 fusion.102
  836.9 12.5 fusion.30
  851.3 94.9 %all-reduce.14.cloned.1.call-done = f32[512,2048]{1,0:T(8,128)} async-done(((f32[512,2048]{1,0:T(8,128)}), f32[512,2048]{1,0:T(8,128)}) %all-reduce.14.cloned.1.call-update) | async-done | bytes 4194320 | tf_op jit(solution)/shard_map/psum | solution.py:256
  949.4 24.0 %all-reduce.2 = (f32[2048]{0:T(1024)S(1)}, f32[2048]{0:T(1024)S(1)}) all-reduce(f32[2048]{0:T(1024)S(1)} %get-tuple-element.70, f32[2048]{0:T(1024)S(1)} %get-tuple-element.68), channel_id=5, replica_groups=mesh['seq'=8,'tp'=4] {'seq'}, use_global_device_ids=true, to_apply=%region_11.13.clone | all-reduce | flops 4096 | bytes 32768
  974.7 7.4 fusion.15
  982.1 18.4 %reduce-scatter.20.cloned.1.call-done = f32[512,256]{1,0:T(8,128)} async-done(((f32[512,2048]{1,0:T(8,128)}), f32[512,256]{1,0:T(8,128)}) %reduce-scatter.20.cloned.1.call-update) | async-done | bytes 524304 | tf_op jit(solution)/shard_map/reduce_scatter | solution.py:277
  1000.5 55.5 %reduce-scatter.18.cloned.1.call-done = f32[256,512]{1,0:T(8,128)} async-done(((f32[2048,512]{1,0:T(8,128)}), f32[256,512]{1,0:T(8,128)}) %reduce-scatter.18.cloned.1.call-update) | async-done | bytes 524304 | tf_op jit(solution)/shard_map/reduce_scatter | solution.py:276
  1056.0 55.3 %reduce-scatter.16.cloned.1.call-done = f32[256,512]{1,0:T(8,128)} async-done(((f32[2048,512]{1,0:T(8,128)}), f32[256,512]{1,0:T(8,128)}) %reduce-scatter.16.cloned.1.call-update) | async-done | bytes 524304 | tf_op jit(solution)/shard_map/reduce_scatter | solution.py:275
  1111.2 55.5 %reduce-scatter.14.cloned.1.call-done = f32[256,512]{1,0:T(8,128)} async-done(((f32[2048,512]{1,0:T(8,128)}), f32[256,512]{1,0:T(8,128)}) %reduce-scatter.14.cloned.1.call-update) | async-done | bytes 524304 | tf_op jit(solution)/shard_map/reduce_scatter | solution.py:274
  1166.8 120.1 %reduce-scatter.22.cloned.1.call-done = f32[256,2048]{1,0:T(8,128)} async-done(((f32[2048,2048]{1,0:T(8,128)}), f32[256,2048]{1,0:T(8,128)}) %reduce-scatter.22.cloned.1.call-update) | async-done | bytes 2097168 | tf_op jit(solution)/shard_map/reduce_scatter | solution.py:279
  1286.9 120.0 %reduce-scatter.24.cloned.1.call-done = f32[256,2048]{1,0:T(8,128)} async-done(((f32[2048,2048]{1,0:T(8,128)}), f32[256,2048]{1,0:T(8,128)}) %reduce-scatter.24.cloned.1.call-update) | async-done | bytes 2097168 | tf_op jit(solution)/shard_map/reduce_scatter | solution.py:280
  1406.9 120.0 %reduce-scatter.26.cloned.1.call-done = f32[2048,256]{1,0:T(8,128)} async-done(((f32[2048,2048]{1,0:T(8,128)}), f32[2048,256]{1,0:T(8,128)}) %reduce-scatter.26.cloned.1.call-update) | async-done | bytes 2097168 | tf_op jit(solution)/shard_map/reduce_scatter | solution.py:281
  (156 shorter events, 117.2 us)
Async XLA Ops:
  7.2 134.1 %copy-start = (bf16[512,2048]{1,0:T(8,128)(2,1)S(1)}, bf16[512,2048]{1,0:T(8,128)(2,1)}, u32[]{:S(2)}) copy-start(bf16[512,2048]{1,0:T(8,128)(2,1)} %param.21) | copy-start | bytes 6291460
  7.2 99.3 %all-gather.4.cloned.1.call-start = ((), (), s32[]{:S(2)}) async-start(), calls=%async_computation.9 | async-start | bytes 4718592 | tf_op jit(solution)/shard_map/all_gather | solution.py:116
  25.0 15.5 %copy-start.22 = (f32[512]{0:T(512)}, f32[512]{0:T(512)S(1)}, u32[]{:S(2)}) copy-start(f32[512]{0:T(512)S(1)} %add_rsqrt_fusion.1) | copy-start | bytes 6148
  25.1 7.8 copy-start.20
  40.5 15.4 %copy-start.2 = (s32[1,4096]{1,0:T(1,128)S(1)}, s32[1,4096]{1,0:T(1,128)}, u32[]{:S(2)}) copy-start(s32[1,4096]{1,0:T(1,128)} %param.27) | copy-start | bytes 49156
  40.5 83.5 %all-gather.6.cloned.1.call-start = ((), (), s32[]{:S(2)}) async-start(), calls=%async_computation.23 | async-start | bytes 4718592 | tf_op jit(solution)/shard_map/all_gather | solution.py:117
  44.9 257.4 %all-reduce.8.cloned.1.call-start = ((), (), s32[]{:S(2)}) async-start(), calls=%async_computation.10 | async-start | bytes 8388608 | tf_op jit(solution)/shard_map/psum | solution.py:136
  55.9 23.1 %copy-start.3 = (s32[1,4096]{1,0:T(1,128)S(1)}, s32[1,4096]{1,0:T(1,128)}, u32[]{:S(2)}) copy-start(s32[1,4096]{1,0:T(1,128)} %param.28) | copy-start | bytes 49156
  144.6 161.2 %copy-start.24 = (f32[2048]{0:T(1024)S(1)}, f32[2048]{0:T(1024)}, u32[]{:S(2)}) copy-start(f32[2048]{0:T(1024)} %param.22) | copy-start | bytes 24580
  144.6 363.5 %all-reduce.12.cloned.1.call-start = ((), (), s32[]{:S(2)}) async-start(), calls=%async_computation.12 | async-start | bytes 8388608 | tf_op jit(solution)/shard_map/psum | solution.py:171
  305.7 12.3 copy-start.6
  305.8 12.3 slice-start
  306.2 11.9 copy-start.14
  306.2 11.9 slice-start.1
  335.9 8.5 copy-start.27
  335.9 8.5 copy-start.26
  354.0 242.5 %all-reduce.10.cloned.1.call-start = ((), (), s32[]{:S(2)}) async-start(), calls=%async_computation.11 | async-start | bytes 4194304 | tf_op jit(solution)/shard_map/psum | solution.py:145
  364.0 345.2 %reduce-scatter.10.cloned.1.call-start = ((), (), s32[]{:S(2)}) async-start(), calls=%async_computation.13 | async-start | bytes 9437184 | tf_op jit(solution)/shard_map/reduce_scatter | solution.py:230
  638.9 145.1 %reduce-scatter.12.cloned.1.call-start = ((), (), s32[]{:S(2)}) async-start(), calls=%async_computation.14 | async-start | bytes 9437184 | tf_op jit(solution)/shard_map/reduce_scatter | solution.py:231
  660.5 48.7 %copy-start.17 = (f32[512,64]{0,1:T(8,128)S(1)}, f32[512,64]{0,1:T(8,128)}, u32[]{:S(2)}) copy-start(f32[512,64]{0,1:T(8,128)} %copy-done.16) | copy-start | bytes 393220
  660.5 48.7 %copy-start.19 = (f32[512,64]{0,1:T(8,128)S(1)}, f32[512,64]{0,1:T(8,128)}, u32[]{:S(2)}) copy-start(f32[512,64]{0,1:T(8,128)} %copy-done.18) | copy-start | bytes 393220
  660.6 285.6 %all-reduce.14.cloned.1.call-start = ((), (), s32[]{:S(2)}) async-start(), calls=%async_computation.15 | async-start | bytes 8388608 | tf_op jit(solution)/shard_map/psum | solution.py:256
  674.3 36.6 %copy-start.8 = (bf16[2048,512]{1,0:T(8,128)(2,1)S(1)}, bf16[2048,512]{1,0:T(8,128)(2,1)}, u32[]{:S(2)}) copy-start(bf16[2048,512]{1,0:T(8,128)(2,1)} %param.19) | copy-start | bytes 6291460
  714.2 69.9 %copy-start.12 = (bf16[2048,512]{1,0:T(8,128)(2,1)S(1)}, bf16[2048,512]{1,0:T(8,128)(2,1)}, u32[]{:S(2)}) copy-start(bf16[2048,512]{1,0:T(8,128)(2,1)} %param.20) | copy-start | bytes 6291460
  791.0 209.4 %reduce-scatter.20.cloned.1.call-start = ((), (), s32[]{:S(2)}) async-start(), calls=%async_computation.19 | async-start | bytes 4718592 | tf_op jit(solution)/shard_map/reduce_scatter | solution.py:277
  797.7 258.3 %reduce-scatter.18.cloned.1.call-start = ((), (), s32[]{:S(2)}) async-start(), calls=%async_computation.18 | async-start | bytes 4718592 | tf_op jit(solution)/shard_map/reduce_scatter | solution.py:276
  803.9 307.3 %reduce-scatter.16.cloned.1.call-start = ((), (), s32[]{:S(2)}) async-start(), calls=%async_computation.17 | async-start | bytes 4718592 | tf_op jit(solution)/shard_map/reduce_scatter | solution.py:275
  807.9 358.9 %reduce-scatter.14.cloned.1.call-start = ((), (), s32[]{:S(2)}) async-start(), calls=%async_computation.16 | async-start | bytes 4718592 | tf_op jit(solution)/shard_map/reduce_scatter | solution.py:274
  811.3 475.5 %reduce-scatter.22.cloned.1.call-start = ((), (), s32[]{:S(2)}) async-start(), calls=%async_computation.20 | async-start | bytes 18874368 | tf_op jit(solution)/shard_map/reduce_scatter | solution.py:279
  824.0 582.8 %reduce-scatter.24.cloned.1.call-start = ((), (), s32[]{:S(2)}) async-start(), calls=%async_computation.21 | async-start | bytes 18874368 | tf_op jit(solution)/shard_map/reduce_scatter | solution.py:280
  836.6 690.2 %reduce-scatter.26.cloned.1.call-start = ((), (), s32[]{:S(2)}) async-start(), calls=%async_computation.22 | async-start | bytes 18874368 | tf_op jit(solution)/shard_map/reduce_scatter | solution.py:281
  974.7 552.1 %copy-start.1 = (bf16[512,2048]{1,0:T(8,128)(2,1)S(1)}, bf16[512,2048]{1,0:T(8,128)(2,1)}, u32[]{:S(2)}) copy-start(bf16[512,2048]{1,0:T(8,128)(2,1)} %param.21) | copy-start | bytes 6291460
  (13 other events, 27.9 us)
Sparse Core Ops, SparseCore 0:
  40.6 40.1 all-gather.3
  83.2 36.7 all-gather.5
  144.7 157.5 all-reduce.7
  354.1 153.9 all-reduce.11
  510.9 85.5 all-reduce.9
  639.0 70.1 reduce-scatter.9
  712.7 71.2 reduce-scatter.11
  791.2 154.9 all-reduce.13
  950.1 50.3 reduce-scatter.19
  1004.6 51.2 reduce-scatter.17
  1059.9 51.2 reduce-scatter.15
  1115.4 51.3 reduce-scatter.13
  1170.9 115.9 reduce-scatter.21
  1290.9 115.9 reduce-scatter.23
  1410.8 115.9 reduce-scatter.25
where the time goes:
time: 1540 us; the launch traced here: 1530 us
  waiting for transfers between devices  1130 us (73%)
  matrix products  241 us (16%)
  local copies, waits for them, and re-layouts  67.8 us (4%)
  other arithmetic  56.7 us (4%)
  blocking collectives  24 us (2%)
    psum x1, waiting for transfers between devices, local(): lax.psum(jnp.dot(attended_flat, w_out, preferred_element_type=jnp.float32...  157 us
    psum x1, waiting for transfers between devices, local(): grad_normed_ffn = lax.psum(normed_ffn_part, 'tp')  144 us
    reduce_scatter x1, waiting for transfers between devices, local(): lax.psum_scatter(grad_gate, 'seq', scatter_dimension=0, tiled=True)  120 us
    reduce_scatter x1, waiting for transfers between devices, local(): lax.psum_scatter(grad_up, 'seq', scatter_dimension=0, tiled=True)  120 us
    reduce_scatter x1, waiting for transfers between devices, local(): lax.psum_scatter(grad_down, 'seq', scatter_dimension=1, tiled=True)  120 us
    psum x1, waiting for transfers between devices, local(): grad_normed_attn = lax.psum(normed_attn_part, 'tp')  94.9 us
    psum x1, waiting for transfers between devices, local(): lax.psum(jnp.dot(activation_rows, w_down, preferred_element_type=jnp.floa...  83.9 us
    reduce_scatter x1, waiting for transfers between devices, local(): lax.psum_scatter(grad_value_all, 'seq', scatter_dimension=1, tiled=True)  66.6 us
  transfers between devices with their start and end apart: 15, of which 13 were waited for; matrix products, arithmetic and copies ran while one was open for 14% of the time, Pallas kernels for 0%

commit v1 on v0

--- a/solution.py
+++ b/solution.py
@@ -142,9 +142,14 @@
     up_projected = jnp.dot(normalized_feedforward, w_up, preferred_element_type=jnp.float32)
     gate_sig = jax.nn.sigmoid(gate_rows)
     activation_rows = (gate_rows * gate_sig * up_projected).astype(jnp.bfloat16)
-    branch_ffn = lax.psum(
-        jnp.dot(activation_rows, w_down, preferred_element_type=jnp.float32).astype(jnp.bfloat16),
-        "tp",
+    branch_ffn = jnp.sum(
+        lax.all_gather(
+            jnp.dot(activation_rows, w_down, preferred_element_type=jnp.float32).astype(
+                jnp.bfloat16
+            ),
+            "tp",
+        ),
+        axis=0,
     ).astype(jnp.float32)
     layer_out = (
         (hidden_rows + branch_ffn).astype(jnp.bfloat16).reshape(seq_count, row_count, model_width)

time: 1540 us -> 1610 us (1.045)
  waiting for transfers between devices: 1130 us -> 1190 us
    all_gather x0 -> x1, waiting for transfers between devices: none -> 146 us  [local(): lax.all_gather(jnp.dot(activation_rows, w_down, preferred_element_type=jn...]
    psum x1 -> x0, waiting for transfers between devices: 83.9 us -> none  [local(): lax.psum(jnp.dot(activation_rows, w_down, preferred_element_type=jnp.floa...]
  transfers between devices with their start and end apart: 15 -> 15, of which waited for: 13 -> 13; matrix products, arithmetic and copies ran while one was open for 14% -> 12% of each run, Pallas kernels for 0% -> 0%
where the time goes in v1:
time: 1610 us; the launch traced here: 1600 us
  waiting for transfers between devices  1190 us (74%)
  matrix products  233 us (14%)
  local copies, waits for them, and re-layouts  70.9 us (4%)
  other arithmetic  64 us (4%)
  blocking collectives  24 us (1%)
    psum x1, waiting for transfers between devices, local(): lax.psum(jnp.dot(attended_flat, w_out, preferred_element_type=jnp.float32...  158 us
    all_gather x1, waiting for transfers between devices, local(): lax.all_gather(jnp.dot(activation_rows, w_down, preferred_element_type=jn...  146 us
    psum x1, waiting for transfers between devices, local(): grad_normed_ffn = lax.psum(normed_ffn_part, 'tp')  144 us
    reduce_scatter x1, waiting for transfers between devices, local(): lax.psum_scatter(grad_up, 'seq', scatter_dimension=0, tiled=True)  120 us
    reduce_scatter x1, waiting for transfers between devices, local(): lax.psum_scatter(grad_down, 'seq', scatter_dimension=1, tiled=True)  120 us
    reduce_scatter x1, waiting for transfers between devices, local(): lax.psum_scatter(grad_gate, 'seq', scatter_dimension=0, tiled=True)  120 us
    psum x1, waiting for transfers between devices, local(): grad_normed_attn = lax.psum(normed_attn_part, 'tp')  101 us
    reduce_scatter x1, waiting for transfers between devices, local(): lax.psum_scatter(grad_value_all, 'seq', scatter_dimension=1, tiled=True)  67 us
  transfers between devices with their start and end apart: 15, of which 13 were waited for; matrix products, arithmetic and copies ran while one was open for 12% of the time, Pallas kernels for 0%

profile of v1, /device:TPU:0, one launch (start us, length us, event | category | flops | bytes accessed | tf_op | source)
XLA Modules:
  0.0 1603.0 jit_solution(7581747670245494147)
XLA Ops:
  56.1 23.0 %gather_fusion.1 = s32[4096]{0:T(1024)S(1)} fusion(s32[4096]{0:T(1024)S(1)} %bitcast.182, s32[4096]{0:T(1024)S(1)} %broadcast_clamp_fusion), kind=kCustom, calls=%fused_computation.clone | custom fusion | bytes 49152 | tf_op jit(solution)/shard_map/jit(take_along_axis)/gather | solution.py:86
  79.1 23.0 %gather_fusion.2 = s32[4096]{0:T(1024)S(1)} fusion(s32[4096]{0:T(1024)S(1)} %bitcast.183, s32[4096]{0:T(1024)S(1)} %broadcast_clamp_fusion), kind=kCustom, calls=%fused_computation.1.clone | custom fusion | bytes 49152 | tf_op jit(solution)/shard_map/jit(take_along_axis)/gather | solution.py:87
  106.7 17.4 %add_divide_fusion = f32[4,512,4096]{2,1,0:T(8,128)} fusion(bf16[4096,4,128]{0,2,1:T(8,128)(2,1)} %bitcast.195, bf16[512,4,64]{0,2,1:T(8,128)(2,1)S(1)} %get-tuple-element.103, bf16[512,4,64]{0,2,1:T(8,128)(2,1)S(1)} %get-tuple-element.102), kind=kOutput, calls=%fused_computation.8 | convolution fusion | flops 2190475264 | bytes 38273024 | tf_op jit(solution)/shard_map/while/body/eval_jaxpr/qhe,khe->hqk/dot_general | solution.py:44
  124.1 16.5 %fusion.56 = bf16[4,128,512]{2,1,0:T(8,128)(2,1)S(1)} fusion(f32[4,512,4096]{2,1,0:T(8,128)} %add_divide_fusion, f32[512,4096]{1,0:T(8,128)} %and_convert_fusion, bf16[4096,512]{1,0:T(8,128)(2,1)} %all-gather.8.cloned.1.call-done), kind=kOutput, calls=%fused_computation.74 | convolution fusion | flops 2164523008 | bytes 46661632 | tf_op jit(solution)/shard_map/while/body/eval_jaxpr/hqk,khe->qhe/dot_general | solution.py:129
  145.0 157.5 %all-reduce.7.cloned.1.call-done = f32[512,2048]{1,0:T(8,128)} async-done(((f32[512,2048]{1,0:T(8,128)}), f32[512,2048]{1,0:T(8,128)}) %all-reduce.7.cloned.1.call-update) | async-done | bytes 4194320 | tf_op jit(solution)/shard_map/psum | solution.py:136
  306.5 11.8 fusion.96
  324.5 11.7 multiply_convert_fusion.1
  336.1 8.5 fusion.98
  344.6 9.5 convolution_add_fusion
  354.7 9.9 convolution_convert_fusion
  364.6 143.7 %all-reduce.9.cloned.1.call-done = f32[512,2048]{1,0:T(8,128)} async-done(((f32[512,2048]{1,0:T(8,128)}), f32[512,2048]{1,0:T(8,128)}) %all-reduce.9.cloned.1.call-update) | async-done | bytes 4194320 | tf_op jit(solution)/shard_map/psum | solution.py:176
  512.8 146.2 %all-gather.10.cloned.1.call-done = bf16[2048,2048]{1,0:T(8,128)(2,1)} async-done(((bf16[512,2048]{1,0:T(8,128)(2,1)}), bf16[2048,2048]{1,0:T(8,128)(2,1)}) %all-gather.10.cloned.1.call-update) | async-done | bytes 8388624 | tf_op jit(solution)/shard_map/all_gather | solution.py:146
  659.0 7.2 reduce_sum.68
  676.1 21.1 %fusion.2 = bf16[4,512,4096]{2,1,0:T(8,128)(2,1)} fusion(f32[4,512,4096]{2,1,0:T(8,128)} %add_divide_fusion, f32[512,4096]{1,0:T(8,128)} %and_convert_fusion, bf16[512,4,128]{0,2,1:T(8,128)(2,1)S(1)} %bitcast.197, bf16[4096,512]{1,0:T(8,128)(2,1)} %all-gather.8.cloned.1.call-done), kind=kOutput, calls=%fused_computation.6 | convolution fusion | flops 2189426688 | bytes 63438848 | tf_op jit(solution)/shard_map/while/body/eval_jaxpr/qhe,khe->hqk/dot_general | solution.py:51
  697.2 11.5 convolution_multiply_fusion
  708.7 21.6 %fusion.26 = f32[4,128,4096]{2,1,0:T(8,128)} fusion(bf16[512,4,128]{0,2,1:T(8,128)(2,1)S(1)} %bitcast.198, f32[4,512,4096]{2,1,0:T(8,128)} %add_divide_fusion, f32[512,4096]{1,0:T(8,128)} %and_convert_fusion), kind=kOutput, calls=%fused_computation.49 | convolution fusion | flops 2164260864 | bytes 50855936 | tf_op jit(solution)/shard_map/while/body/eval_jaxpr/hqk,qhe->khe/dot_general | solution.py:203
  730.6 13.5 fusion.52
  744.0 34.3 %reduce-scatter.10.cloned.1.call-done = f32[1,512,512]{1,2,0:T(8,128)} async-done(((f32[1,4096,512]{1,2,0:T(8,128)}), f32[1,512,512]{1,2,0:T(8,128)}) %reduce-scatter.10.cloned.1.call-update) | async-done | bytes 1048592 | tf_op jit(solution)/shard_map/reduce_scatter | solution.py:235
  786.4 67.0 %reduce-scatter.12.cloned.1.call-done = f32[1,512,512]{1,2,0:T(8,128)} async-done(((f32[1,4096,512]{1,2,0:T(8,128)}), f32[1,512,512]{1,2,0:T(8,128)}) %reduce-scatter.12.cloned.1.call-update) | async-done | bytes 1048592 | tf_op jit(solution)/shard_map/reduce_scatter | solution.py:236
  868.7 9.8 fusion.101
  878.8 9.8 fusion.102
  890.2 9.7 fusion.30
  915.1 100.6 %all-reduce.11.cloned.1.call-done = f32[512,2048]{1,0:T(8,128)} async-done(((f32[512,2048]{1,0:T(8,128)}), f32[512,2048]{1,0:T(8,128)}) %all-reduce.11.cloned.1.call-update) | async-done | bytes 4194320 | tf_op jit(solution)/shard_map/psum | solution.py:261
  1018.9 24.0 %all-reduce.2 = (f32[2048]{0:T(1024)S(1)}, f32[2048]{0:T(1024)S(1)}) all-reduce(f32[2048]{0:T(1024)S(1)} %get-tuple-element.70, f32[2048]{0:T(1024)S(1)} %get-tuple-element.68), channel_id=6, replica_groups=mesh['seq'=8,'tp'=4] {'seq'}, use_global_device_ids=true, to_apply=%region_11.13.clone | all-reduce | flops 4096 | bytes 32768
  1044.2 7.3 fusion.15
  1051.5 18.8 %reduce-scatter.20.cloned.1.call-done = f32[512,256]{1,0:T(8,128)} async-done(((f32[512,2048]{1,0:T(8,128)}), f32[512,256]{1,0:T(8,128)}) %reduce-scatter.20.cloned.1.call-update) | async-done | bytes 524304 | tf_op jit(solution)/shard_map/reduce_scatter | solution.py:282
  1070.3 120.0 %reduce-scatter.22.cloned.1.call-done = f32[256,2048]{1,0:T(8,128)} async-done(((f32[2048,2048]{1,0:T(8,128)}), f32[256,2048]{1,0:T(8,128)}) %reduce-scatter.22.cloned.1.call-update) | async-done | bytes 2097168 | tf_op jit(solution)/shard_map/reduce_scatter | solution.py:284
  1190.2 120.1 %reduce-scatter.24.cloned.1.call-done = f32[256,2048]{1,0:T(8,128)} async-done(((f32[2048,2048]{1,0:T(8,128)}), f32[256,2048]{1,0:T(8,128)}) %reduce-scatter.24.cloned.1.call-update) | async-done | bytes 2097168 | tf_op jit(solution)/shard_map/reduce_scatter | solution.py:285
  1310.4 120.0 %reduce-scatter.26.cloned.1.call-done = f32[2048,256]{1,0:T(8,128)} async-done(((f32[2048,2048]{1,0:T(8,128)}), f32[2048,256]{1,0:T(8,128)}) %reduce-scatter.26.cloned.1.call-update) | async-done | bytes 2097168 | tf_op jit(solution)/shard_map/reduce_scatter | solution.py:286
  1430.3 55.3 %reduce-scatter.18.cloned.1.call-done = f32[256,512]{1,0:T(8,128)} async-done(((f32[2048,512]{1,0:T(8,128)}), f32[256,512]{1,0:T(8,128)}) %reduce-scatter.18.cloned.1.call-update) | async-done | bytes 524304 | tf_op jit(solution)/shard_map/reduce_scatter | solution.py:281
  1485.6 55.5 %reduce-scatter.16.cloned.1.call-done = f32[256,512]{1,0:T(8,128)} async-done(((f32[2048,512]{1,0:T(8,128)}), f32[256,512]{1,0:T(8,128)}) %reduce-scatter.16.cloned.1.call-update) | async-done | bytes 524304 | tf_op jit(solution)/shard_map/reduce_scatter | solution.py:280
  1541.2 55.1 %reduce-scatter.14.cloned.1.call-done = f32[256,512]{1,0:T(8,128)} async-done(((f32[2048,512]{1,0:T(8,128)}), f32[256,512]{1,0:T(8,128)}) %reduce-scatter.14.cloned.1.call-update) | async-done | bytes 524304 | tf_op jit(solution)/shard_map/reduce_scatter | solution.py:279
  (161 shorter events, 126.9 us)
Async XLA Ops:
  7.2 134.3 %copy-start = (bf16[512,2048]{1,0:T(8,128)(2,1)S(1)}, bf16[512,2048]{1,0:T(8,128)(2,1)}, u32[]{:S(2)}) copy-start(bf16[512,2048]{1,0:T(8,128)(2,1)} %param.21) | copy-start | bytes 6291460
  7.2 99.5 %all-gather.6.cloned.1.call-start = ((), (), s32[]{:S(2)}) async-start(), calls=%async_computation.9 | async-start | bytes 4718592 | tf_op jit(solution)/shard_map/all_gather | solution.py:116
  25.0 15.5 copy-start.24
  25.1 7.8 copy-start.22
  40.5 15.6 copy-start.2
  40.5 83.6 %all-gather.8.cloned.1.call-start = ((), (), s32[]{:S(2)}) async-start(), calls=%async_computation.22 | async-start | bytes 4718592 | tf_op jit(solution)/shard_map/all_gather | solution.py:117
  44.9 257.6 %all-reduce.7.cloned.1.call-start = ((), (), s32[]{:S(2)}) async-start(), calls=%async_computation.10 | async-start | bytes 8388608 | tf_op jit(solution)/shard_map/psum | solution.py:136
  56.1 23.1 %copy-start.3 = (s32[1,4096]{1,0:T(1,128)S(1)}, s32[1,4096]{1,0:T(1,128)}, u32[]{:S(2)}) copy-start(s32[1,4096]{1,0:T(1,128)} %param.28) | copy-start | bytes 49156
  144.7 161.3 %copy-start.26 = (f32[2048]{0:T(1024)S(1)}, f32[2048]{0:T(1024)}, u32[]{:S(2)}) copy-start(f32[2048]{0:T(1024)} %param.22) | copy-start | bytes 24580
  144.8 363.6 %all-reduce.9.cloned.1.call-start = ((), (), s32[]{:S(2)}) async-start(), calls=%async_computation.11 | async-start | bytes 8388608 | tf_op jit(solution)/shard_map/psum | solution.py:176
  306.0 12.3 copy-start.6
  306.0 12.3 slice-start
  306.4 11.9 copy-start.15
  306.5 11.9 slice-start.1
  336.1 8.5 copy-start.29
  336.1 8.5 copy-start.28
  354.2 304.8 %all-gather.10.cloned.1.call-start = ((), (), s32[]{:S(2)}) async-start(), calls=%async_computation.23 | async-start | bytes 10485760 | tf_op jit(solution)/shard_map/all_gather | solution.py:146
  364.5 413.8 %reduce-scatter.10.cloned.1.call-start = ((), (), s32[]{:S(2)}) async-start(), calls=%async_computation.12 | async-start | bytes 9437184 | tf_op jit(solution)/shard_map/reduce_scatter | solution.py:235
  708.7 144.8 %reduce-scatter.12.cloned.1.call-start = ((), (), s32[]{:S(2)}) async-start(), calls=%async_computation.13 | async-start | bytes 9437184 | tf_op jit(solution)/shard_map/reduce_scatter | solution.py:236
  730.3 48.0 %copy-start.19 = (f32[512,64]{0,1:T(8,128)S(1)}, f32[512,64]{0,1:T(8,128)}, u32[]{:S(2)}) copy-start(f32[512,64]{0,1:T(8,128)} %copy-done.18) | copy-start | bytes 393220
  730.3 48.0 %copy-start.21 = (f32[512,64]{0,1:T(8,128)S(1)}, f32[512,64]{0,1:T(8,128)}, u32[]{:S(2)}) copy-start(f32[512,64]{0,1:T(8,128)} %copy-done.20) | copy-start | bytes 393220
  730.4 285.3 %all-reduce.11.cloned.1.call-start = ((), (), s32[]{:S(2)}) async-start(), calls=%async_computation.14 | async-start | bytes 8388608 | tf_op jit(solution)/shard_map/psum | solution.py:261
  744.0 35.9 %copy-start.8 = (bf16[2048,512]{1,0:T(8,128)(2,1)S(1)}, bf16[2048,512]{1,0:T(8,128)(2,1)}, u32[]{:S(2)}) copy-start(bf16[2048,512]{1,0:T(8,128)(2,1)} %param.19) | copy-start | bytes 6291460
  783.2 70.3 %copy-start.12 = (bf16[2048,512]{1,0:T(8,128)(2,1)S(1)}, bf16[2048,512]{1,0:T(8,128)(2,1)}, u32[]{:S(2)}) copy-start(bf16[2048,512]{1,0:T(8,128)(2,1)} %param.20) | copy-start | bytes 6291460
  860.5 209.8 %reduce-scatter.20.cloned.1.call-start = ((), (), s32[]{:S(2)}) async-start(), calls=%async_computation.18 | async-start | bytes 4718592 | tf_op jit(solution)/shard_map/reduce_scatter | solution.py:282
  867.1 323.1 %reduce-scatter.22.cloned.1.call-start = ((), (), s32[]{:S(2)}) async-start(), calls=%async_computation.19 | async-start | bytes 18874368 | tf_op jit(solution)/shard_map/reduce_scatter | solution.py:284
  878.5 431.9 %reduce-scatter.24.cloned.1.call-start = ((), (), s32[]{:S(2)}) async-start(), calls=%async_computation.20 | async-start | bytes 18874368 | tf_op jit(solution)/shard_map/reduce_scatter | solution.py:285
  888.6 541.7 %reduce-scatter.26.cloned.1.call-start = ((), (), s32[]{:S(2)}) async-start(), calls=%async_computation.21 | async-start | bytes 18874368 | tf_op jit(solution)/shard_map/reduce_scatter | solution.py:286
  899.9 585.8 %reduce-scatter.18.cloned.1.call-start = ((), (), s32[]{:S(2)}) async-start(), calls=%async_computation.17 | async-start | bytes 4718592 | tf_op jit(solution)/shard_map/reduce_scatter | solution.py:281
  906.2 635.0 %reduce-scatter.16.cloned.1.call-start = ((), (), s32[]{:S(2)}) async-start(), calls=%async_computation.16 | async-start | bytes 4718592 | tf_op jit(solution)/shard_map/reduce_scatter | solution.py:280
  909.7 686.6 %reduce-scatter.14.cloned.1.call-start = ((), (), s32[]{:S(2)}) async-start(), calls=%async_computation.15 | async-start | bytes 4718592 | tf_op jit(solution)/shard_map/reduce_scatter | solution.py:279
  1044.2 552.1 %copy-start.1 = (bf16[512,2048]{1,0:T(8,128)(2,1)S(1)}, bf16[512,2048]{1,0:T(8,128)(2,1)}, u32[]{:S(2)}) copy-start(bf16[512,2048]{1,0:T(8,128)(2,1)} %param.21) | copy-start | bytes 6291460
  (15 other events, 31.3 us)
Sparse Core Ops, SparseCore 0:
  40.6 40.1 all-gather.5
  83.2 36.7 all-gather.7
  144.9 157.5 all-reduce.6
  354.3 153.9 all-reduce.8
  510.3 148.6 all-gather.9
  708.8 69.4 reduce-scatter.9
  782.2 71.2 reduce-scatter.11
  860.6 154.9 all-reduce.10
  1019.9 50.3 reduce-scatter.19
  1074.3 115.9 reduce-scatter.21
  1194.4 115.9 reduce-scatter.23
  1314.4 115.9 reduce-scatter.25
  1434.3 51.3 reduce-scatter.17
  1489.8 51.3 reduce-scatter.15
  1544.9 51.2 reduce-scatter.13
